TPU v7x, 512 devices: a whole 4x4x16 slice. The times are simulated.
512 devices in a mesh: group: 32 (over x, y, core), tp: 16 (over z).
Axes of the slice: x: 4, y: 4, z: 16, core: 2. Of those that a mesh axis runs over, the one named last changes fastest.
Arguments:
- tokens: bfloat16 [24576, 8192], P('group', 'tp'), may hold values from -6 to 6
- w_query: bfloat16 [8192, 4096], P(None, 'tp'), may hold values from -0.0625 to 0.0625
- adapter_down: bfloat16 [384, 16, 8192], P('group', None, 'tp'), may hold values from -0.0625 to 0.0625
- adapter_up: bfloat16 [384, 16, 4096], P('group', None, 'tp'), may hold values from -1.5 to 1.5
- adapter_id: int32 [24576], P('group'), may hold values from 0 to 383, as said below
Outputs:
- query: bfloat16 [24576, 4096], P('group', 'tp')
Inputs may be any that keep to these rules, and one draw needn't show every extreme that they name: `adapter_id`: adapter a is owned by group a // 12. Among the 768 requests of one group (an aligned block), at most 48 use adapters of any one owner; in every draw one owner receives exactly 48 from every group.
All inputs are finite; a program needn't handle non-finite values.
Results may differ from a plain program's by a relative error of at most 0.014.
Values may be sent and summed in bfloat16 or wider, within the bound.
No kernel may reach another device: no remote copies, remote signals or barrier semaphores. Data moves between devices by JAX's collectives and lax.ppermute only.
A program may use at most 128 MiB of HBM per device.

v0:
```python
import jax
import jax.numpy as jnp
from jax import lax
from jax.sharding import PartitionSpec as P

adapter_scale_factor = 2.0


def on_device(tokens, w_query, adapter_down, adapter_up, adapter_id):
    pool_down, pool_up = (
        lax.all_gather(adapter_down, "group", axis=0, tiled=True),
        lax.all_gather(adapter_up, "group", axis=0, tiled=True),
    )
    picked_down = jnp.take(pool_down, adapter_id, axis=0)
    partial_value = jnp.einsum(
        "nd,nrd->nr", tokens, picked_down, preferred_element_type=jnp.float32
    )
    total_output = lax.psum(partial_value, "tp")
    scaled_delta = (adapter_scale_factor * total_output).astype(jnp.bfloat16)
    picked_up = jnp.take(pool_up, adapter_id, axis=0)
    delta_rows = jnp.einsum(
        "nr,nrh->nh", scaled_delta, picked_up, preferred_element_type=jnp.float32
    ).astype(jnp.bfloat16)
    base = jnp.dot(
        lax.all_gather(tokens, "tp", axis=1, tiled=True),
        w_query,
        preferred_element_type=jnp.float32,
    )
    return (base + delta_rows.astype(jnp.float32)).astype(jnp.bfloat16)


def solution(mesh):
    placed = (
        P("group", "tp"),
        P(None, "tp"),
        P("group", None, "tp"),
        P("group", None, "tp"),
        P("group"),
    )
    return jax.shard_map(
        on_device, mesh=mesh, in_specs=placed, out_specs=P("group", "tp"), check_vma=False
    )
```

profile of v0, /device:TPU:1, one launch (start us, length us, event | category | flops | bytes accessed | tf_op | source)
XLA Modules:
  0.0 317.1 jit_solution(11295828361454792933)
XLA Ops:
  6.5 0.0 all-gather.8.cloned.1.call-start
  6.5 0.7 all-gather.8.cloned.1.call-update
  7.3 0.0 all-gather.6.cloned.1.call-start
  7.3 0.7 all-gather.6.cloned.1.call-update
  8.0 0.0 all-gather.4.cloned.1.call-start
  8.1 0.7 all-gather.4.cloned.1.call-update
  8.7 0.7 compare_select_fusion
  9.4 0.7 compare_and_fusion
  10.1 66.6 %all-gather.8.cloned.1.call-done = bf16[384,16,256]{2,1,0:T(8,128)(2,1)} async-done(((bf16[12,16,256]{2,1,0:T(8,128)(2,1)}), bf16[384,16,256]{2,1,0:T(8,128)(2,1)}) %all-gather.8.cloned.1.call-update) | async-done | bytes 3145744 | tf_op jit(solution)/shard_map/all_gather | solution.py:12
  76.7 7.0 %gather_fusion.1 = bf16[768,16,256]{2,1,0:T(8,128)(2,1)} fusion(bf16[384,16,256]{2,1,0:T(8,128)(2,1)} %all-gather.8.cloned.1.call-done, s32[1024]{0:T(1024)S(1)} %pad_clamp_fusion), kind=kCustom, calls=%fused_computation.1 | custom fusion | bytes 12585984 | tf_op jit(solution)/shard_map/jit(_take)/gather | solution.py:20
  83.6 0.0 copy-start
  83.6 60.0 %all-gather.6.cloned.1.call-done = bf16[384,16,512]{2,1,0:T(8,128)(2,1)} async-done(((bf16[12,16,512]{2,1,0:T(8,128)(2,1)}), bf16[384,16,512]{2,1,0:T(8,128)(2,1)}) %all-gather.6.cloned.1.call-update) | async-done | bytes 6291472 | tf_op jit(solution)/shard_map/all_gather | solution.py:11
  143.7 22.4 %gather_fusion = bf16[768,16,512]{2,1,0:T(8,128)(2,1)} fusion(bf16[384,16,512]{2,1,0:T(8,128)(2,1)} %all-gather.6.cloned.1.call-done, s32[1024]{0:T(1024)S(1)} %pad_clamp_fusion), kind=kCustom, calls=%fused_computation | custom fusion | bytes 25168896 | tf_op jit(solution)/shard_map/jit(_take)/gather | solution.py:14
  166.1 0.0 copy-done
  166.1 9.9 %fusion = f32[768,1,16]{2,1,0:T(1,128)S(1)} fusion(bf16[768,16,512]{2,1,0:T(8,128)(2,1)} %gather_fusion, pred[768]{0:T(1024)(128)(4,1)S(1)} %compare_and_fusion, bf16[768,512,1]{1,0,2:T(8,128)(2,1)S(1)} %bitcast.11), kind=kOutput, calls=%fused_computation.2 | convolution fusion | flops 18874368 | bytes 13419264 | tf_op jit(solution)/shard_map/nd,nrd->nr/dot_general | solution.py:15
  176.1 61.4 %psum.7 = f32[768,16]{1,0:T(8,128)S(1)} all-reduce(f32[768,16]{1,0:T(8,128)S(1)} %bitcast.12), channel_id=1, replica_groups=mesh['group'=32,'tp'=16] {'tp'}, use_global_device_ids=true, to_apply=%region_0.1 | all-reduce | flops 12288 | bytes 98304 | tf_op jit(solution)/shard_map/psum | solution.py:18
  237.5 8.5 %fusion.3 = bf16[768,1,256]{2,1,0:T(2,128)(2,1)S(1)} fusion(bf16[768,16,256]{2,1,0:T(8,128)(2,1)} %gather_fusion.1, pred[768]{0:T(1024)(128)(4,1)S(1)} %compare_and_fusion, bf16[768,16,1]{1,0,2:T(8,128)(2,1)S(1)} %fusion.11), kind=kOutput, calls=%fused_computation.5 | convolution fusion | flops 9437184 | bytes 6710016 | tf_op jit(solution)/shard_map/nr,nrh->nh/dot_general | solution.py:21
  246.0 54.7 %all-gather.4.cloned.1.call-done = bf16[768,8192]{1,0:T(8,128)(2,1)} async-done(((bf16[768,512]{1,0:T(8,128)(2,1)}), bf16[768,8192]{1,0:T(8,128)(2,1)}) %all-gather.4.cloned.1.call-update) | async-done | bytes 12582928 | tf_op jit(solution)/shard_map/all_gather | solution.py:25
  300.7 9.9 %fusion.9 = bf16[768,256]{1,0:T(8,128)(2,1)} fusion(bf16[768,8192]{1,0:T(8,128)(2,1)} %all-gather.4.cloned.1.call-done, bf16[8192,256]{1,0:T(8,128)(2,1)} %param.6, bf16[768,1,256]{2,1,0:T(2,128)(2,1)S(1)} %fusion.3), kind=kOutput, calls=%fused_computation.12 | convolution fusion | flops 3221815296 | bytes 17563648 | tf_op jit(solution)/shard_map/dot_general | solution.py:24
  (2 shorter events, 0.0 us)
Async XLA Ops:
  6.5 70.2 %all-gather.8.cloned.1.call-start = ((), (), s32[]{:S(2)}) async-start(), calls=%async_computation.2 | async-start | bytes 3244032 | tf_op jit(solution)/shard_map/all_gather | solution.py:12
  7.3 136.4 %all-gather.6.cloned.1.call-start = ((), (), s32[]{:S(2)}) async-start(), calls=%async_computation.1 | async-start | bytes 6488064 | tf_op jit(solution)/shard_map/all_gather | solution.py:11
  8.0 292.7 %all-gather.4.cloned.1.call-start = ((), (), s32[]{:S(2)}) async-start(), calls=%async_computation | async-start | bytes 13369344 | tf_op jit(solution)/shard_map/all_gather | solution.py:25
  83.6 82.5 %copy-start = (bf16[768,512]{1,0:T(8,128)(2,1)S(1)}, bf16[768,512]{1,0:T(8,128)(2,1)}, u32[]{:S(2)}) copy-start(bf16[768,512]{1,0:T(8,128)(2,1)} %param.5) | copy-start | bytes 2359300
Sparse Core Ops, SparseCore 0:
  10.5 66.1 all-gather.7
  79.8 63.8 all-gather.5
  145.8 154.8 all-gather.3
where the time goes:
time: 317 us
  waiting for transfers between devices  183 us (58%)
  blocking collectives  61.4 us (19%)
  local copies, waits for them, and re-layouts  29.4 us (9%)
  matrix products  28.3 us (9%)
  between operations  13.2 us (4%)
    all_gather x1, waiting for transfers between devices, on_device(): lax.all_gather(adapter_up, 'group', axis=0, tiled=True)  66.6 us
    psum x1, blocking collectives, on_device(): total_output = lax.psum(partial_value, 'tp')  61.4 us
    all_gather x1, waiting for transfers between devices, on_device(): lax.all_gather(adapter_down, 'group', axis=0, tiled=True)  60 us
    all_gather x1, waiting for transfers between devices, on_device(): lax.all_gather(tokens, 'tp', axis=1, tiled=True)  54.7 us
    gather x1, local copies, waits for them, and re-layouts, on_device(): picked_down = jnp.take(pool_down, adapter_id, axis=0)  22.4 us
    dot_general x1, matrix products, on_device(): jnp.dot(lax.all_gather(tokens, 'tp', axis=1, tiled=True), w_query, prefer...  9.92 us
    dot_general x1, matrix products, on_device(): jnp.einsum('nd,nrd->nr', tokens, picked_down, preferred_element_type=jnp....  9.91 us
    dot_general x1, matrix products, on_device(): jnp.einsum('nr,nrh->nh', scaled_delta, picked_up, preferred_element_type=...  8.51 us
  transfers between devices with their start and end apart: 3, of which 3 were waited for; matrix products, arithmetic and copies ran while one was open for 16% of the time, Pallas kernels for 0%

commit v1 on v0

--- a/solution.py
+++ b/solution.py
@@ -4,6 +4,27 @@
 from jax.sharding import PartitionSpec as P
 
 adapter_scale_factor = 2.0
+
+
+def collect(array, axis, dim):
+    size, place, width = (lax.axis_size(axis), lax.axis_index(axis), array.shape[dim])
+    right = [(i, (i + 1) % size) for i in range(size)]
+    left = [(i, (i - 1) % size) for i in range(size)]
+    out = jnp.zeros((*array.shape[:dim], size * width, *array.shape[dim + 1 :]), array.dtype)
+    out = lax.dynamic_update_slice_in_dim(out, array, place * width, axis=dim)
+    from_left = from_right = array
+    halfway = size // 2
+    for turn in range(1, halfway + 1):
+        from_left = lax.ppermute(from_left, axis, right)
+        out = lax.dynamic_update_slice_in_dim(
+            out, from_left, (place - turn) % size * width, axis=dim
+        )
+        if turn < size - halfway:
+            from_right = lax.ppermute(from_right, axis, left)
+            out = lax.dynamic_update_slice_in_dim(
+                out, from_right, (place + turn) % size * width, axis=dim
+            )
+    return out
 
 
 def on_device(tokens, w_query, adapter_down, adapter_up, adapter_id):
@@ -21,11 +42,7 @@
     delta_rows = jnp.einsum(
         "nr,nrh->nh", scaled_delta, picked_up, preferred_element_type=jnp.float32
     ).astype(jnp.bfloat16)
-    base = jnp.dot(
-        lax.all_gather(tokens, "tp", axis=1, tiled=True),
-        w_query,
-        preferred_element_type=jnp.float32,
-    )
+    base = jnp.dot(collect(tokens, "tp", 1), w_query, preferred_element_type=jnp.float32)
     return (base + delta_rows.astype(jnp.float32)).astype(jnp.bfloat16)
 
 

time: 317 us -> 291 us (0.918)
  the two profiles are of different devices: /device:TPU:1 before, /device:TPU:24 now
where the time goes in v1:
time: 291 us; the launch traced here: 290 us
  waiting for transfers between devices  75.6 us (26%)
  blocking collectives  60 us (21%)
  starting transfers between devices  58.1 us (20%)
  local copies, waits for them, and re-layouts  55.8 us (19%)
  matrix products  25.9 us (9%)
  between operations  13.7 us (5%)
    ppermute x8, waiting for transfers between devices, collect(): from_left = lax.ppermute(from_left, axis, right)  70.9 us
    psum x1, blocking collectives, on_device(): total_output = lax.psum(partial_value, 'tp')  60 us
    ppermute x7, starting transfers between devices, collect(): from_right = lax.ppermute(from_right, axis, left)  40.7 us
    gather x1, local copies, waits for them, and re-layouts, on_device(): picked_down = jnp.take(pool_down, adapter_id, axis=0)  22.4 us
    ppermute x8, starting transfers between devices, collect(): from_left = lax.ppermute(from_left, axis, right)  17.4 us
    dynamic_update_slice x8, local copies, waits for them, and re-layouts, collect(): lax.dynamic_update_slice_in_dim(out, from_left, (place - turn) % size * w...  10.1 us
    dot_general x1, matrix products, on_device(): jnp.einsum('nd,nrd->nr', tokens, picked_down, preferred_element_type=jnp....  9.89 us
    dynamic_update_slice x7, local copies, waits for them, and re-layouts, collect(): lax.dynamic_update_slice_in_dim(out, from_right, (place + turn) % size *...  9.18 us
  transfers between devices with their start and end apart: 17, of which 8 were waited for; matrix products, arithmetic and copies ran while one was open for 12% of the time, Pallas kernels for 0%

profile of v1, /device:TPU:24, one launch (start us, length us, event | category | flops | bytes accessed | tf_op | source)
XLA Modules:
  0.0 289.9 jit_solution(10413746270445385759)
XLA Ops:
  6.5 0.0 all-gather.5.cloned.1.call-start
  6.5 0.7 all-gather.5.cloned.1.call-update
  7.3 0.0 all-gather.3.cloned.1.call-start
  7.3 0.7 all-gather.3.cloned.1.call-update
  8.0 3.8 %collective-permute-start = (bf16[768,512]{1,0:T(8,128)(2,1)}, bf16[768,512]{1,0:T(8,128)(2,1)S(1)}, u32[]{:S(2)}, u32[]{:S(2)}) collective-permute-start(bf16[768,512]{1,0:T(8,128)(2,1)} %param.5), channel_id=1, source_target_pairs={{0,1},{1,2},{2,3},{3,4},{4,5},{5,6},{6,7},{7,8},{8,9},{9,10},{10,1... | collective-permute-start | bytes 2359304 | tf_op jit(solution)/shard_map/ppermute | solution.py:18
  11.8 9.5 %collective-permute-start.1 = (bf16[768,512]{1,0:T(8,128)(2,1)}, bf16[768,512]{1,0:T(8,128)(2,1)S(1)}, u32[]{:S(2)}, u32[]{:S(2)}) collective-permute-start(bf16[768,512]{1,0:T(8,128)(2,1)} %param.5), channel_id=1, source_target_pairs={{0,15},{1,0},{2,1},{3,2},{4,3},{5,4},{6,5},{7,6},{8,7},{9,8},{10,9... | collective-permute-start | bytes 2359304 | tf_op jit(solution)/shard_map/ppermute | solution.py:23
  21.3 15.8 %collective-permute-done = bf16[768,512]{1,0:T(8,128)(2,1)S(1)} collective-permute-done((bf16[768,512]{1,0:T(8,128)(2,1)}, bf16[768,512]{1,0:T(8,128)(2,1)S(1)}, u32[]{:S(2)}, u32[]{:S(2)}) %collective-permute-start) | collective-permute-done | bytes 786464 | tf_op jit(solution)/shard_map/ppermute | solution.py:18
  37.2 1.9 collective-permute-start.2
  39.1 0.0 collective-permute-done.1
  39.1 5.1 %collective-permute-start.3 = (bf16[768,512]{1,0:T(8,128)(2,1)S(1)}, bf16[768,512]{1,0:T(8,128)(2,1)S(1)}, u32[]{:S(2)}, u32[]{:S(2)}) collective-permute-start(bf16[768,512]{1,0:T(8,128)(2,1)S(1)} %collective-permute-done.1), channel_id=1, source_target_pairs={{0,15},{1,0},{2,1},{3,2},{4,3},{5,4},{6,5},{7,6},{8,7},{9,8},{10,9... | collective-permute-start | bytes 2359304 | tf_op jit(solution)/shard_map/ppermute | solution.py:23
  44.2 0.0 copy-done.5
  44.2 14.7 %collective-permute-done.2 = bf16[768,512]{1,0:T(8,128)(2,1)S(1)} collective-permute-done((bf16[768,512]{1,0:T(8,128)(2,1)S(1)}, bf16[768,512]{1,0:T(8,128)(2,1)S(1)}, u32[]{:S(2)}, u32[]{:S(2)}) %collective-permute-start.2) | collective-permute-done | bytes 786464 | tf_op jit(solution)/shard_map/ppermute | solution.py:18
  59.0 1.9 collective-permute-start.4
  60.9 0.0 collective-permute-done.3
  60.9 5.1 %collective-permute-start.5 = (bf16[768,512]{1,0:T(8,128)(2,1)S(1)}, bf16[768,512]{1,0:T(8,128)(2,1)S(1)}, u32[]{:S(2)}, u32[]{:S(2)}) collective-permute-start(bf16[768,512]{1,0:T(8,128)(2,1)S(1)} %collective-permute-done.3), channel_id=1, source_target_pairs={{0,15},{1,0},{2,1},{3,2},{4,3},{5,4},{6,5},{7,6},{8,7},{9,8},{10,9... | collective-permute-start | bytes 2359304 | tf_op jit(solution)/shard_map/ppermute | solution.py:23
  66.0 13.8 %collective-permute-done.4 = bf16[768,512]{1,0:T(8,128)(2,1)S(1)} collective-permute-done((bf16[768,512]{1,0:T(8,128)(2,1)S(1)}, bf16[768,512]{1,0:T(8,128)(2,1)S(1)}, u32[]{:S(2)}, u32[]{:S(2)}) %collective-permute-start.4) | collective-permute-done | bytes 786464 | tf_op jit(solution)/shard_map/ppermute | solution.py:18
  79.9 1.9 collective-permute-start.6
  81.8 0.0 collective-permute-done.5
  81.8 0.0 copy-done.1
  81.8 0.0 copy-start.3
  81.8 5.1 %collective-permute-start.7 = (bf16[768,512]{1,0:T(8,128)(2,1)S(1)}, bf16[768,512]{1,0:T(8,128)(2,1)}, u32[]{:S(2)}, u32[]{:S(2)}) collective-permute-start(bf16[768,512]{1,0:T(8,128)(2,1)S(1)} %collective-permute-done.5), channel_id=1, source_target_pairs={{0,15},{1,0},{2,1},{3,2},{4,3},{5,4},{6,5},{7,6},{8,7},{9,8},{10,9... | collective-permute-start | bytes 2359304 | tf_op jit(solution)/shard_map/ppermute | solution.py:23
  87.0 12.9 %collective-permute-done.6 = bf16[768,512]{1,0:T(8,128)(2,1)S(1)} collective-permute-done((bf16[768,512]{1,0:T(8,128)(2,1)S(1)}, bf16[768,512]{1,0:T(8,128)(2,1)S(1)}, u32[]{:S(2)}, u32[]{:S(2)}) %collective-permute-start.6) | collective-permute-done | bytes 786464 | tf_op jit(solution)/shard_map/ppermute | solution.py:18
  99.9 1.9 collective-permute-start.8
  101.8 0.0 collective-permute-done.7
  101.8 5.1 %collective-permute-start.9 = (bf16[768,512]{1,0:T(8,128)(2,1)}, bf16[768,512]{1,0:T(8,128)(2,1)}, u32[]{:S(2)}, u32[]{:S(2)}) collective-permute-start(bf16[768,512]{1,0:T(8,128)(2,1)} %collective-permute-done.7), channel_id=1, source_target_pairs={{0,15},{1,0},{2,1},{3,2},{4,3},{5,4},{6,5},{7,6},{8,7},{9,8},{10,9... | collective-permute-start | bytes 2359304 | tf_op jit(solution)/shard_map/ppermute | solution.py:23
  106.9 12.1 %collective-permute-done.8 = bf16[768,512]{1,0:T(8,128)(2,1)} collective-permute-done((bf16[768,512]{1,0:T(8,128)(2,1)S(1)}, bf16[768,512]{1,0:T(8,128)(2,1)}, u32[]{:S(2)}, u32[]{:S(2)}) %collective-permute-start.8) | collective-permute-done | bytes 786464 | tf_op jit(solution)/shard_map/ppermute | solution.py:18
  119.0 1.9 collective-permute-start.10
  120.9 0.7 compare_select_fusion
  121.7 6.1 %broadcast_in_dim.25 = bf16[768,8192]{1,0:T(8,128)(2,1)} broadcast(bf16[]{:T(256)} %constant.114.clone.1), dimensions={} | broadcast | bytes 12582914 | tf_op jit(solution)/shard_map/broadcast_in_dim | solution.py:13
  127.7 1.0 constant_dynamic-update-slice_fusion.15
  128.7 0.0 copy-done.9
  128.7 0.9 constant_dynamic-update-slice_fusion.14
  129.7 0.0 collective-permute-done.9
  129.7 5.3 %collective-permute-start.11 = (bf16[768,512]{1,0:T(8,128)(2,1)}, bf16[768,512]{1,0:T(8,128)(2,1)S(1)}, u32[]{:S(2)}, u32[]{:S(2)}) collective-permute-start(bf16[768,512]{1,0:T(8,128)(2,1)} %collective-permute-done.9), channel_id=1, source_target_pairs={{0,15},{1,0},{2,1},{3,2},{4,3},{5,4},{6,5},{7,6},{8,7},{9,8},{10,9... | collective-permute-start | bytes 2359304 | tf_op jit(solution)/shard_map/ppermute | solution.py:23
  135.0 1.0 constant_dynamic-update-slice_fusion.13
  136.0 1.5 collective-permute-done.10
  137.5 1.9 collective-permute-start.12
  139.4 1.0 constant_dynamic-update-slice_fusion.12
  140.4 1.0 constant_dynamic-update-slice_fusion.11
  141.3 1.0 constant_dynamic-update-slice_fusion.10
  142.3 0.0 copy-done.4
  142.3 1.0 constant_dynamic-update-slice_fusion.9
  143.3 1.0 constant_dynamic-update-slice_fusion.8
  144.3 3.3 %collective-permute-done.11 = bf16[768,512]{1,0:T(8,128)(2,1)S(1)} collective-permute-done((bf16[768,512]{1,0:T(8,128)(2,1)}, bf16[768,512]{1,0:T(8,128)(2,1)S(1)}, u32[]{:S(2)}, u32[]{:S(2)}) %collective-permute-start.11) | collective-permute-done | bytes 786464 | tf_op jit(solution)/shard_map/ppermute | solution.py:23
  147.6 5.4 %collective-permute-start.13 = (bf16[768,512]{1,0:T(8,128)(2,1)S(1)}, bf16[768,512]{1,0:T(8,128)(2,1)S(1)}, u32[]{:S(2)}, u32[]{:S(2)}) collective-permute-start(bf16[768,512]{1,0:T(8,128)(2,1)S(1)} %collective-permute-done.11), channel_id=1, source_target_pairs={{0,15},{1,0},{2,1},{3,2},{4,3},{5,4},{6,5},{7,6},{8,7},{9,8},{10,9... | collective-permute-start | bytes 2359304 | tf_op jit(solution)/shard_map/ppermute | solution.py:23
  152.9 2.1 constant_dynamic-update-slice_fusion.7
  155.1 0.1 collective-permute-done.12
  155.2 2.1 collective-permute-start.14
  157.3 2.1 constant_dynamic-update-slice_fusion.6
  159.4 2.1 constant_dynamic-update-slice_fusion.5
  161.5 2.2 constant_dynamic-update-slice_fusion.4
  163.7 1.0 constant_dynamic-update-slice_fusion.3
  164.7 1.0 constant_dynamic-update-slice_fusion.2
  165.7 0.0 collective-permute-done.13
  165.7 1.0 constant_dynamic-update-slice_fusion.1
  166.7 7.0 %gather_fusion.1 = bf16[768,16,256]{2,1,0:T(8,128)(2,1)} fusion(bf16[384,16,256]{2,1,0:T(8,128)(2,1)} %all-gather.5.cloned.1.call-done, s32[1024]{0:T(1024)S(1)} %pad_clamp_fusion), kind=kCustom, calls=%fused_computation.1 | custom fusion | bytes 12585984 | tf_op jit(solution)/shard_map/jit(_take)/gather | solution.py:41
  173.6 0.0 collective-permute-done.14
  173.6 1.0 constant_dynamic-update-slice_fusion
  174.6 22.4 %gather_fusion = bf16[768,16,512]{2,1,0:T(8,128)(2,1)} fusion(bf16[384,16,512]{2,1,0:T(8,128)(2,1)} %all-gather.3.cloned.1.call-done, s32[1024]{0:T(1024)S(1)} %pad_clamp_fusion), kind=kCustom, calls=%fused_computation | custom fusion | bytes 25168896 | tf_op jit(solution)/shard_map/jit(_take)/gather | solution.py:35
  197.1 9.9 %fusion = f32[768,1,16]{2,1,0:T(1,128)S(1)} fusion(bf16[768,16,512]{2,1,0:T(8,128)(2,1)} %gather_fusion, pred[768]{0:T(1024)(128)(4,1)S(1)} %compare_and_fusion, bf16[768,512,1]{1,0,2:T(8,128)(2,1)S(1)} %bitcast.11), kind=kOutput, calls=%fused_computation.2 | convolution fusion | flops 18874368 | bytes 13419264 | tf_op jit(solution)/shard_map/nd,nrd->nr/dot_general | solution.py:36
  207.0 60.0 %psum.7 = f32[768,16]{1,0:T(8,128)S(1)} all-reduce(f32[768,16]{1,0:T(8,128)S(1)} %bitcast.12), channel_id=1, replica_groups=mesh['group'=32,'tp'=16] {'tp'}, use_global_device_ids=true, to_apply=%region_0.1 | all-reduce | flops 12288 | bytes 98304 | tf_op jit(solution)/shard_map/psum | solution.py:39
  267.0 0.0 copy-start.10
  267.0 8.7 %fusion.3 = bf16[768,1,256]{2,1,0:T(2,128)(2,1)S(1)} fusion(bf16[768,16,256]{2,1,0:T(8,128)(2,1)} %gather_fusion.1, pred[768]{0:T(1024)(128)(4,1)S(1)} %compare_and_fusion, bf16[768,16,1]{1,0,2:T(8,128)(2,1)S(1)} %fusion.11), kind=kOutput, calls=%fused_computation.5 | convolution fusion | flops 9437184 | bytes 6710016 | tf_op jit(solution)/shard_map/nr,nrh->nh/dot_general | solution.py:42
  275.7 7.3 %fusion.9 = bf16[768,256]{1,0:T(8,128)(2,1)} fusion(bf16[768,8192]{1,0:T(8,128)(2,1)} %constant_dynamic-update-slice_fusion, bf16[8192,256]{1,0:T(8,128)(2,1)S(1)} %copy-done.10, bf16[768,1,256]{2,1,0:T(2,128)(2,1)S(1)} %fusion.3), kind=kOutput, calls=%fused_computation.12 | convolution fusion | flops 3221815296 | bytes 17563648 | tf_op jit(solution)/shard_map/dot_general | solution.py:45
  (21 shorter events, 0.1 us)
Async XLA Ops:
  6.5 121.2 %copy-start = (bf16[768,512]{1,0:T(8,128)(2,1)S(1)}, bf16[768,512]{1,0:T(8,128)(2,1)}, u32[]{:S(2)}) copy-start(bf16[768,512]{1,0:T(8,128)(2,1)} %param.5) | copy-start | bytes 2359300
  6.5 122.2 %copy-start.9 = (s32[768]{0:T(1024)S(1)}, s32[768]{0:T(1024)}, u32[]{:S(2)}) copy-start(s32[768]{0:T(1024)} %param.9) | copy-start | bytes 9220
  6.5 160.1 %all-gather.5.cloned.1.call-start = ((), (), s32[]{:S(2)}) async-start(), calls=%async_computation.1 | async-start | bytes 3244032 | tf_op jit(solution)/shard_map/all_gather | solution.py:33
  7.3 167.4 %all-gather.3.cloned.1.call-start = ((), (), s32[]{:S(2)}) async-start(), calls=%async_computation | async-start | bytes 6488064 | tf_op jit(solution)/shard_map/all_gather | solution.py:32
  8.0 29.1 %collective-permute-start = (bf16[768,512]{1,0:T(8,128)(2,1)}, bf16[768,512]{1,0:T(8,128)(2,1)S(1)}, u32[]{:S(2)}, u32[]{:S(2)}) collective-permute-start(bf16[768,512]{1,0:T(8,128)(2,1)} %param.5), channel_id=1, source_target_pairs={{0,1},{1,2},{2,3},{3,4},{4,5},{5,6},{6,7},{7,8},{8,9},{9,10},{10,1... | collective-permute-start | bytes 2359304 | tf_op jit(solution)/shard_map/ppermute | solution.py:18
  11.8 27.2 %collective-permute-start.1 = (bf16[768,512]{1,0:T(8,128)(2,1)}, bf16[768,512]{1,0:T(8,128)(2,1)S(1)}, u32[]{:S(2)}, u32[]{:S(2)}) collective-permute-start(bf16[768,512]{1,0:T(8,128)(2,1)} %param.5), channel_id=1, source_target_pairs={{0,15},{1,0},{2,1},{3,2},{4,3},{5,4},{6,5},{7,6},{8,7},{9,8},{10,9... | collective-permute-start | bytes 2359304 | tf_op jit(solution)/shard_map/ppermute | solution.py:23
  37.2 7.1 %copy-start.5 = (bf16[768,512]{1,0:T(8,128)(2,1)}, bf16[768,512]{1,0:T(8,128)(2,1)S(1)}, u32[]{:S(2)}) copy-start(bf16[768,512]{1,0:T(8,128)(2,1)S(1)} %collective-permute-done) | copy-start | bytes 2359300
  37.2 21.8 %collective-permute-start.2 = (bf16[768,512]{1,0:T(8,128)(2,1)S(1)}, bf16[768,512]{1,0:T(8,128)(2,1)S(1)}, u32[]{:S(2)}, u32[]{:S(2)}) collective-permute-start(bf16[768,512]{1,0:T(8,128)(2,1)S(1)} %collective-permute-done), channel_id=1, source_target_pairs={{0,1},{1,2},{2,3},{3,4},{4,5},{5,6},{6,7},{7,8},{8,9},{9,10},{10,1... | collective-permute-start | bytes 2359304 | tf_op jit(solution)/shard_map/ppermute | solution.py:18
  39.1 21.8 %collective-permute-start.3 = (bf16[768,512]{1,0:T(8,128)(2,1)S(1)}, bf16[768,512]{1,0:T(8,128)(2,1)S(1)}, u32[]{:S(2)}, u32[]{:S(2)}) collective-permute-start(bf16[768,512]{1,0:T(8,128)(2,1)S(1)} %collective-permute-done.1), channel_id=1, source_target_pairs={{0,15},{1,0},{2,1},{3,2},{4,3},{5,4},{6,5},{7,6},{8,7},{9,8},{10,9... | collective-permute-start | bytes 2359304 | tf_op jit(solution)/shard_map/ppermute | solution.py:23
  59.0 20.9 %collective-permute-start.4 = (bf16[768,512]{1,0:T(8,128)(2,1)S(1)}, bf16[768,512]{1,0:T(8,128)(2,1)S(1)}, u32[]{:S(2)}, u32[]{:S(2)}) collective-permute-start(bf16[768,512]{1,0:T(8,128)(2,1)S(1)} %collective-permute-done.2), channel_id=1, source_target_pairs={{0,1},{1,2},{2,3},{3,4},{4,5},{5,6},{6,7},{7,8},{8,9},{9,10},{10,1... | collective-permute-start | bytes 2359304 | tf_op jit(solution)/shard_map/ppermute | solution.py:18
  60.9 20.9 %collective-permute-start.5 = (bf16[768,512]{1,0:T(8,128)(2,1)S(1)}, bf16[768,512]{1,0:T(8,128)(2,1)S(1)}, u32[]{:S(2)}, u32[]{:S(2)}) collective-permute-start(bf16[768,512]{1,0:T(8,128)(2,1)S(1)} %collective-permute-done.3), channel_id=1, source_target_pairs={{0,15},{1,0},{2,1},{3,2},{4,3},{5,4},{6,5},{7,6},{8,7},{9,8},{10,9... | collective-permute-start | bytes 2359304 | tf_op jit(solution)/shard_map/ppermute | solution.py:23
  79.9 1.9 copy-start.1
  79.9 20.0 %collective-permute-start.6 = (bf16[768,512]{1,0:T(8,128)(2,1)S(1)}, bf16[768,512]{1,0:T(8,128)(2,1)S(1)}, u32[]{:S(2)}, u32[]{:S(2)}) collective-permute-start(bf16[768,512]{1,0:T(8,128)(2,1)S(1)} %collective-permute-done.4), channel_id=1, source_target_pairs={{0,1},{1,2},{2,3},{3,4},{4,5},{5,6},{6,7},{7,8},{8,9},{9,10},{10,1... | collective-permute-start | bytes 2359304 | tf_op jit(solution)/shard_map/ppermute | solution.py:18
  81.8 18.0 %copy-start.3 = (bf16[768,512]{1,0:T(8,128)(2,1)}, bf16[768,512]{1,0:T(8,128)(2,1)S(1)}, u32[]{:S(2)}) copy-start(bf16[768,512]{1,0:T(8,128)(2,1)S(1)} %collective-permute-done.5) | copy-start | bytes 2359300
  81.8 20.0 %collective-permute-start.7 = (bf16[768,512]{1,0:T(8,128)(2,1)S(1)}, bf16[768,512]{1,0:T(8,128)(2,1)}, u32[]{:S(2)}, u32[]{:S(2)}) collective-permute-start(bf16[768,512]{1,0:T(8,128)(2,1)S(1)} %collective-permute-done.5), channel_id=1, source_target_pairs={{0,15},{1,0},{2,1},{3,2},{4,3},{5,4},{6,5},{7,6},{8,7},{9,8},{10,9... | collective-permute-start | bytes 2359304 | tf_op jit(solution)/shard_map/ppermute | solution.py:23
  99.9 1.9 copy-start.7
  99.9 19.2 %collective-permute-start.8 = (bf16[768,512]{1,0:T(8,128)(2,1)S(1)}, bf16[768,512]{1,0:T(8,128)(2,1)}, u32[]{:S(2)}, u32[]{:S(2)}) collective-permute-start(bf16[768,512]{1,0:T(8,128)(2,1)S(1)} %collective-permute-done.6), channel_id=1, source_target_pairs={{0,1},{1,2},{2,3},{3,4},{4,5},{5,6},{6,7},{7,8},{8,9},{9,10},{10,1... | collective-permute-start | bytes 2359304 | tf_op jit(solution)/shard_map/ppermute | solution.py:18
  101.8 27.9 %collective-permute-start.9 = (bf16[768,512]{1,0:T(8,128)(2,1)}, bf16[768,512]{1,0:T(8,128)(2,1)}, u32[]{:S(2)}, u32[]{:S(2)}) collective-permute-start(bf16[768,512]{1,0:T(8,128)(2,1)} %collective-permute-done.7), channel_id=1, source_target_pairs={{0,15},{1,0},{2,1},{3,2},{4,3},{5,4},{6,5},{7,6},{8,7},{9,8},{10,9... | collective-permute-start | bytes 2359304 | tf_op jit(solution)/shard_map/ppermute | solution.py:23
  119.0 18.5 %collective-permute-start.10 = (bf16[768,512]{1,0:T(8,128)(2,1)}, bf16[768,512]{1,0:T(8,128)(2,1)}, u32[]{:S(2)}, u32[]{:S(2)}) collective-permute-start(bf16[768,512]{1,0:T(8,128)(2,1)} %collective-permute-done.8), channel_id=1, source_target_pairs={{0,1},{1,2},{2,3},{3,4},{4,5},{5,6},{6,7},{7,8},{8,9},{9,10},{10,1... | collective-permute-start | bytes 2359304 | tf_op jit(solution)/shard_map/ppermute | solution.py:18
  121.6 7.1 %copy-start.6 = (bf16[768,512]{1,0:T(8,128)(2,1)S(1)}, bf16[768,512]{1,0:T(8,128)(2,1)}, u32[]{:S(2)}) copy-start(bf16[768,512]{1,0:T(8,128)(2,1)} %copy-done.5) | copy-start | bytes 2359300
  121.6 19.7 %copy-start.2 = (bf16[768,512]{1,0:T(8,128)(2,1)S(1)}, bf16[768,512]{1,0:T(8,128)(2,1)}, u32[]{:S(2)}) copy-start(bf16[768,512]{1,0:T(8,128)(2,1)} %copy-done.1) | copy-start | bytes 2359300
  121.6 20.7 %copy-start.4 = (bf16[768,512]{1,0:T(8,128)(2,1)S(1)}, bf16[768,512]{1,0:T(8,128)(2,1)}, u32[]{:S(2)}) copy-start(bf16[768,512]{1,0:T(8,128)(2,1)} %copy-done.3) | copy-start | bytes 2359300
  121.6 21.7 %copy-start.8 = (bf16[768,512]{1,0:T(8,128)(2,1)S(1)}, bf16[768,512]{1,0:T(8,128)(2,1)}, u32[]{:S(2)}) copy-start(bf16[768,512]{1,0:T(8,128)(2,1)} %copy-done.7) | copy-start | bytes 2359300
  129.7 17.9 %collective-permute-start.11 = (bf16[768,512]{1,0:T(8,128)(2,1)}, bf16[768,512]{1,0:T(8,128)(2,1)S(1)}, u32[]{:S(2)}, u32[]{:S(2)}) collective-permute-start(bf16[768,512]{1,0:T(8,128)(2,1)} %collective-permute-done.9), channel_id=1, source_target_pairs={{0,15},{1,0},{2,1},{3,2},{4,3},{5,4},{6,5},{7,6},{8,7},{9,8},{10,9... | collective-permute-start | bytes 2359304 | tf_op jit(solution)/shard_map/ppermute | solution.py:23
  137.5 17.7 %collective-permute-start.12 = (bf16[768,512]{1,0:T(8,128)(2,1)}, bf16[768,512]{1,0:T(8,128)(2,1)S(1)}, u32[]{:S(2)}, u32[]{:S(2)}) collective-permute-start(bf16[768,512]{1,0:T(8,128)(2,1)} %collective-permute-done.10), channel_id=1, source_target_pairs={{0,1},{1,2},{2,3},{3,4},{4,5},{5,6},{6,7},{7,8},{8,9},{9,10},{10,1... | collective-permute-start | bytes 2359304 | tf_op jit(solution)/shard_map/ppermute | solution.py:18
  147.6 18.1 %collective-permute-start.13 = (bf16[768,512]{1,0:T(8,128)(2,1)S(1)}, bf16[768,512]{1,0:T(8,128)(2,1)S(1)}, u32[]{:S(2)}, u32[]{:S(2)}) collective-permute-start(bf16[768,512]{1,0:T(8,128)(2,1)S(1)} %collective-permute-done.11), channel_id=1, source_target_pairs={{0,15},{1,0},{2,1},{3,2},{4,3},{5,4},{6,5},{7,6},{8,7},{9,8},{10,9... | collective-permute-start | bytes 2359304 | tf_op jit(solution)/shard_map/ppermute | solution.py:23
  155.2 18.5 %collective-permute-start.14 = (bf16[768,512]{1,0:T(8,128)(2,1)S(1)}, bf16[768,512]{1,0:T(8,128)(2,1)S(1)}, u32[]{:S(2)}, u32[]{:S(2)}) collective-permute-start(bf16[768,512]{1,0:T(8,128)(2,1)S(1)} %collective-permute-done.12), channel_id=1, source_target_pairs={{0,1},{1,2},{2,3},{3,4},{4,5},{5,6},{6,7},{7,8},{8,9},{9,10},{10,1... | collective-permute-start | bytes 2359304 | tf_op jit(solution)/shard_map/ppermute | solution.py:18
  267.0 8.7 %copy-start.10 = (bf16[8192,256]{1,0:T(8,128)(2,1)S(1)}, bf16[8192,256]{1,0:T(8,128)(2,1)}, u32[]{:S(2)}) copy-start(bf16[8192,256]{1,0:T(8,128)(2,1)} %param.6) | copy-start | bytes 12582916
Sparse Core Ops, SparseCore 0:
  10.5 64.1 all-gather.4
  77.8 63.4 all-gather.2
